TPU v7x, 128 devices: a whole 4x4x4 slice. The times are simulated.
128 devices in a mesh: row: 8 (over x, y_hi), col: 16 (over y_lo, z, core).
Axes of the slice: x: 4, y: 4 (y_hi: 2, y_lo: 2; y = y_hi * 2 + y_lo), z: 4, core: 2. Of those that a mesh axis runs over, the one named last changes fastest.
Arguments:
- train_inputs: bfloat16 [512, 8192], P(('row', 'col')), may hold values from -6 to 6
- train_grads: bfloat16 [512, 8192], P(('row', 'col')), may hold values from -6 to 6
- query_inputs: bfloat16 [256, 8192], P(('row', 'col')), may hold values from -6 to 6
- query_grads: bfloat16 [256, 8192], P(('row', 'col')), may hold values from -6 to 6
- input_basis: bfloat16 [8192, 8192], P('row', 'col'), may hold values from -0.0625 to 0.0625
- output_basis: bfloat16 [8192, 8192], P('col', 'row'), may hold values from -0.0625 to 0.0625
- eigenvalues: float32 [8192, 8192], P('row', 'col'), may hold values from 0.5 to 5
- query_starts: int32 [16], replicated, may hold values from 0 to 255, as said below
- query_ends: int32 [16], replicated, may hold values from 1 to 256, as said below
Outputs:
- scores: float32 [16, 512], replicated
Inputs may be any that keep to these rules, and one draw needn't show every extreme that they name: Query q covers the query rows query_starts[q] <= r < query_ends[q]: a nonempty span of at most 128 rows that lies inside one aligned block of 128 rows (rows k * 128 to (k + 1) * 128 - 1); spans of different queries may intersect or share a block. `query_ends`: see query_starts.
All inputs are finite; a program needn't handle non-finite values.
Results may differ from a plain program's by a relative error of at most 0.005.
Values may be sent and summed in bfloat16 or wider, within the bound.
A program may use at most 64 MiB of HBM per device.

v0:
```python
import math
import jax
import jax.numpy as jnp
from jax import lax
from jax.sharding import Mesh
from jax.sharding import PartitionSpec as P

D_IN = 8192
D_OUT = 8192
QBLOCK = 128
COL = ("col_0", "col_1", "col_2")
ROW = ("row_0", "row_1")
ROW_COL = ("row_0", "row_1", "col_0", "col_1", "col_2")
damping = 0.1


def laid_out(parts, dim):
    parts = jnp.moveaxis(parts, 0, dim)
    dims = parts.shape
    return parts.reshape(*dims[:dim], dims[dim] * dims[dim + 1], *dims[dim + 2 :])


def gather_together(arrays, axis, dims):
    line = jnp.concatenate([a.reshape(-1) for a in arrays])
    lines, at, gathered = (lax.all_gather(line, axis), 0, [])
    for a, dim in zip(arrays, dims):
        parts = lines[:, at : at + a.size].reshape(-1, *a.shape)
        gathered.append(laid_out(parts, dim))
        at += a.size
    return tuple(gathered)


def by_axis(value, axes):
    for axis in axes:
        value = lax.psum(value, axis)
    return value


def shards(
    train_inputs,
    train_grads,
    query_inputs,
    query_grads,
    input_basis,
    output_basis,
    eigenvalues,
    query_starts,
    query_ends,
):
    grouped = gather_together((train_inputs, query_inputs), COL, (0, 0))
    train_in, query_in = (
        lax.all_to_all(grouped[0], ROW, split_axis=1, concat_axis=0, tiled=True),
        lax.all_to_all(grouped[1], ROW, split_axis=1, concat_axis=0, tiled=True),
    )
    spread = (
        lax.all_to_all(train_grads, COL, split_axis=1, concat_axis=0, tiled=True),
        lax.all_to_all(query_grads, COL, split_axis=1, concat_axis=0, tiled=True),
    )
    train_out, query_out = gather_together((spread[0], spread[1]), ROW, (0, 0))
    train_in_part = jnp.dot(train_in, input_basis, preferred_element_type=jnp.float32)
    query_in_part = jnp.dot(query_in, input_basis, preferred_element_type=jnp.float32)
    train_out_part = jnp.dot(train_out, output_basis, preferred_element_type=jnp.float32)
    query_out_part = jnp.dot(query_out, output_basis, preferred_element_type=jnp.float32)
    in_sums = lax.psum((train_in_part, query_in_part), ROW)
    out_sums = lax.psum((train_out_part, query_out_part), COL)
    train_in_rot = in_sums[0].astype(jnp.bfloat16)
    query_in_rot = in_sums[1].astype(jnp.bfloat16)
    train_grad_rot = out_sums[0].astype(jnp.bfloat16)
    query_grad_rot = out_sums[1].astype(jnp.bfloat16)
    grads_wide = train_grad_rot.astype(jnp.float32)
    denominator = eigenvalues + damping

    def per_query(span):
        span_start, span_end = span
        block_top = span_start // QBLOCK * QBLOCK
        grad_rows = lax.dynamic_slice_in_dim(query_grad_rot, block_top, QBLOCK, 0)
        input_rows = lax.dynamic_slice_in_dim(query_in_rot, block_top, QBLOCK, 0)
        positions = block_top + jnp.arange(QBLOCK, dtype=jnp.int32)
        inside = (positions >= span_start) & (positions < span_end)
        grad_rows = jnp.where(inside[:, None], grad_rows, jnp.zeros((), grad_rows.dtype))
        outer_sum = lax.dot_general(
            grad_rows, input_rows, (((0,), (0,)), ((), ())), preferred_element_type=jnp.float32
        )
        scaled = (outer_sum / denominator).astype(jnp.bfloat16)
        paired = lax.dot_general(
            train_in_rot, scaled, (((1,), (1,)), ((), ())), preferred_element_type=jnp.float32
        )
        return jnp.sum(grads_wide * paired, axis=1)

    partial_scores = lax.map(per_query, (query_starts, query_ends))
    totals = by_axis(partial_scores, ROW_COL)
    return totals * (1.0 / math.sqrt(D_IN * D_OUT * QBLOCK))


def solution(mesh):
    split = Mesh(mesh.devices.reshape(4, 2, 2, 4, 2), ("row_0", "row_1", "col_0", "col_1", "col_2"))
    placed = (
        P(ROW_COL, None),
        P(ROW_COL, None),
        P(ROW_COL, None),
        P(ROW_COL, None),
        P(ROW, COL),
        P(COL, ROW),
        P(ROW, COL),
        P(),
        P(),
    )
    return jax.shard_map(shards, mesh=split, in_specs=placed, out_specs=P(), check_vma=False)
```

profile of v0, /device:TPU:1, one launch (start us, length us, event | category | flops | bytes accessed | tf_op | source)
XLA Modules:
  0.0 458.6 jit_solution(13673715249605043826)
XLA Ops:
  6.5 0.9 copy.26
  7.5 0.8 copy.27
  8.2 0.6 pad_maximum_fusion.1
  8.9 13.6 %all_to_all.70 = bf16[2,16,512]{2,0,1:T(2,128)(2,1)S(1)} all-to-all(bf16[2,16,512]{2,0,1:T(2,128)(2,1)} %bitcast.54), channel_id=1, replica_groups=mesh['row_0'=4,'row_1'=2,'col_0'=2,'col_1'=4,'col_2'=2] {'col_0','col_1'..., dimensions={1} | all-to-all | bytes 65536 | tf_op jit(solution)/shard_map/all_to_all | solution.py:57
  22.6 3.7 all-to-all-start
  26.2 3.2 broadcast_add_fusion
  29.5 2.7 all-to-all-done
  32.2 31.4 %all-gather = bf16[393216]{0:T(1024)(128)(2,1)S(1)} all-gather(bf16[49152]{0:T(1024)(128)(2,1)S(1)} %pad_maximum_fusion), channel_id=2, replica_groups=mesh['row_0'=4,'row_1'=2,'col_0'=2,'col_1'=4,'col_2'=2] {'row_0','row_1'}, dimensions={0}, use_global_device_ids=true | all-gather | bytes 884736 | tf_op jit(solution)/shard_map/all_gather | solution.py:25
  64.0 1.0 reshape_reshape.9
  65.0 1.8 reshape.40
  66.9 0.9 slice.17
  67.7 1.3 all_to_all.58
  69.0 1.1 copy.21
  70.1 4.5 all-to-all-start.2
  74.7 1.8 fusion.18
  76.4 0.8 reshape_reshape.8
  77.3 2.5 fusion.15
  79.7 1.1 slice.18
  80.8 2.3 all_to_all.62
  83.1 2.8 copy.22
  85.9 6.6 %all-to-all-start.3 = ((bf16[64,8,1024]{2,0,1:T(8,128)(2,1)}), bf16[64,8,1024]{2,0,1:T(8,128)(2,1)}, u32[]{:S(2)}, u32[]{:S(2)}) async-start(bf16[64,8,1024]{2,0,1:T(8,128)(2,1)} %copy.22), calls=%async_computation.3 | async-start | bytes 2097152 | tf_op jit(solution)/shard_map/all_to_all | solution.py:52
  92.6 74.4 %all-reduce.4 = (bf16[256,1024]{1,0:T(8,128)(2,1)}, bf16[512,1024]{1,0:T(8,128)(2,1)}) all-reduce(f32[256,1024]{1,0:T(8,128)} %fusion.15, f32[512,1024]{1,0:T(8,128)S(1)} %fusion.18), channel_id=1, replica_groups=mesh['row_0'=4,'row_1'=2,'col_0'=2,'col_1'=4,'col_2'=2] {'col_0','col_1'..., use_global_device_ids=true, to_apply=%region_0.0 | all-reduce | flops 786432 | bytes 4718592 | tf_op jit(solution)/shard_map/psum | solution.py:65
  166.9 1.5 copy.23
  168.4 2.6 fusion.16
  171.0 3.3 fusion.17
  174.3 81.4 %all-reduce.5 = (bf16[256,512]{1,0:T(8,128)(2,1)}, bf16[512,512]{1,0:T(8,128)(2,1)}) all-reduce(f32[256,512]{1,0:T(8,128)} %fusion.16, f32[512,512]{1,0:T(8,128)} %fusion.17), channel_id=1, replica_groups=mesh['row_0'=4,'row_1'=2,'col_0'=2,'col_1'=4,'col_2'=2] {'row_0','row_1'}, use_global_device_ids=true, to_apply=%region_1.0 | all-reduce | flops 393216 | bytes 2359296 | tf_op jit(solution)/shard_map/psum | solution.py:64
  255.7 127.2 %while.12 = (s32[]{:T(128)}, f32[16,512]{1,0:T(8,128)S(1)}, s32[16]{0:T(128)S(1)}, s32[16]{0:T(128)S(1)}, bf16[256,1024]{1,0:T(8,128)(2,1)}, /*index=5*/bf16[256...) while((s32[]{:T(128)}, f32[16,512]{1,0:T(8,128)S(1)}, ...), condition=%wide.region_6.7_spmd, body=%wide.region_4.6_spmd.sunk | while | flops 673316864 | bytes 5119617 | solution.py:90
  259.4 1.2 compare_and_fusion.2
  260.6 2.9 fusion.35
  267.4 1.2 compare_and_fusion.2
  268.6 2.9 fusion.35
  275.3 1.2 compare_and_fusion.2
  276.6 2.9 fusion.35
  283.3 1.2 compare_and_fusion.2
  284.5 2.9 fusion.35
  291.2 1.2 compare_and_fusion.2
  292.5 2.9 fusion.35
  299.2 1.2 compare_and_fusion.2
  300.4 2.9 fusion.35
  307.1 1.2 compare_and_fusion.2
  308.4 2.9 fusion.35
  315.1 1.2 compare_and_fusion.2
  316.3 2.9 fusion.35
  323.0 1.2 compare_and_fusion.2
  324.3 2.9 fusion.35
  331.0 1.2 compare_and_fusion.2
  332.2 2.9 fusion.35
  338.9 1.2 compare_and_fusion.2
  340.2 2.9 fusion.35
  346.9 1.2 compare_and_fusion.2
  348.1 2.9 fusion.35
  354.9 1.2 compare_and_fusion.2
  356.1 2.9 fusion.35
  362.8 1.2 compare_and_fusion.2
  364.0 2.9 fusion.35
  370.8 1.2 compare_and_fusion.2
  372.0 2.9 fusion.35
  378.7 1.2 compare_and_fusion.2
  380.0 2.9 fusion.35
  383.0 11.8 %psum.67 = f32[16,512]{1,0:T(8,128)S(1)} all-reduce(f32[16,512]{1,0:T(8,128)S(1)} %get-tuple-element.119), channel_id=1, replica_groups=mesh['row_0'=4,'row_1'=2,'col_0'=2,'col_1'=4,'col_2'=2] {'row_0'}, use_global_device_ids=true, to_apply=%region_7.8 | all-reduce | flops 8192 | bytes 65536 | tf_op jit(solution)/shard_map/psum | solution.py:35
  394.8 7.5 %psum.68 = f32[16,512]{1,0:T(8,128)S(1)} all-reduce(f32[16,512]{1,0:T(8,128)S(1)} %psum.67), channel_id=1, replica_groups=mesh['row_0'=4,'row_1'=2,'col_0'=2,'col_1'=4,'col_2'=2] {'row_1'}, use_global_device_ids=true, to_apply=%region_8.9 | all-reduce | flops 8192 | bytes 65536 | tf_op jit(solution)/shard_map/psum | solution.py:35
  402.3 6.6 %psum.69 = f32[16,512]{1,0:T(8,128)S(1)} all-reduce(f32[16,512]{1,0:T(8,128)S(1)} %psum.68), channel_id=1, replica_groups=mesh['row_0'=4,'row_1'=2,'col_0'=2,'col_1'=4,'col_2'=2] {'col_0'}, use_global_device_ids=true, to_apply=%region_9.10 | all-reduce | flops 8192 | bytes 65536 | tf_op jit(solution)/shard_map/psum | solution.py:35
  409.0 18.8 %psum.70 = f32[16,512]{1,0:T(8,128)S(1)} all-reduce(f32[16,512]{1,0:T(8,128)S(1)} %psum.69), channel_id=1, replica_groups=mesh['row_0'=4,'row_1'=2,'col_0'=2,'col_1'=4,'col_2'=2] {'col_1'}, use_global_device_ids=true, to_apply=%region_10.11 | all-reduce | flops 8192 | bytes 65536 | tf_op jit(solution)/shard_map/psum | solution.py:35
  427.7 23.4 %psum.71 = f32[16,512]{1,0:T(8,128)S(1)} all-reduce(f32[16,512]{1,0:T(8,128)S(1)} %psum.70), channel_id=1, replica_groups=mesh['row_0'=4,'row_1'=2,'col_0'=2,'col_1'=4,'col_2'=2] {'col_2'}, use_global_device_ids=true, to_apply=%region_11.12 | all-reduce | flops 8192 | bytes 65536 | tf_op jit(solution)/shard_map/psum | solution.py:35
  (74 shorter events, 21.5 us)
Async XLA Ops:
  6.5 68.1 %copy-start = (bf16[512,1024]{1,0:T(8,128)(2,1)S(1)}, bf16[512,1024]{1,0:T(8,128)(2,1)}, u32[]{:S(2)}) copy-start(bf16[512,1024]{1,0:T(8,128)(2,1)} %param.16) | copy-start | bytes 3145732
  6.5 58.5 %all-gather.4.cloned.1.call-start = ((), (), s32[]{:S(2)}) async-start(), calls=%async_computation.4 | async-start | bytes 1671168 | tf_op jit(solution)/shard_map/all_gather | solution.py:25
  22.6 9.6 %all-to-all-start = ((bf16[4,16,512]{2,0,1:T(4,128)(2,1)}), bf16[4,16,512]{2,0,1:T(4,128)(2,1)S(1)}, u32[]{:S(2)}, u32[]{:S(2)}) async-start(bf16[4,16,512]{2,0,1:T(4,128)(2,1)} %bitcast.51), calls=%async_computation | async-start | bytes 131072 | tf_op jit(solution)/shard_map/all_to_all | solution.py:56
  63.9 1.1 copy-start.3
  66.8 3.3 copy-start.1
  70.1 6.3 %slice-start = ((bf16[8,49152]{1,0:T(8,128)(2,1)}), bf16[8,16384]{1,0:T(8,128)(2,1)S(1)}, s32[]{:S(2)}) async-start(bf16[8,49152]{1,0:T(8,128)(2,1)} %copy-done.3), calls=%async_computation.5 | async-start | bytes 524288 | tf_op jit(solution)/shard_map/slice | solution.py:27
  70.1 15.8 %all-to-all-start.2 = ((bf16[32,8,1024]{2,0,1:T(8,128)(2,1)}), bf16[32,8,1024]{2,0,1:T(8,128)(2,1)}, u32[]{:S(2)}, u32[]{:S(2)}) async-start(bf16[32,8,1024]{2,0,1:T(8,128)(2,1)} %copy.21), calls=%async_computation.2 | async-start | bytes 1048576 | tf_op jit(solution)/shard_map/all_to_all | solution.py:53
  77.2 2.5 copy-start.2
  85.9 85.1 %all-to-all-start.3 = ((bf16[64,8,1024]{2,0,1:T(8,128)(2,1)}), bf16[64,8,1024]{2,0,1:T(8,128)(2,1)}, u32[]{:S(2)}, u32[]{:S(2)}) async-start(bf16[64,8,1024]{2,0,1:T(8,128)(2,1)} %copy.22), calls=%async_computation.3 | async-start | bytes 2097152 | tf_op jit(solution)/shard_map/all_to_all | solution.py:52
  171.0 84.7 %copy-start.4 = (s32[16]{0:T(128)S(1)}, s32[16]{0:T(128)}, u32[]{:S(2)}) copy-start(s32[16]{0:T(128)} %param.18) | copy-start | bytes 196
  171.0 84.7 %copy-start.5 = (s32[16]{0:T(128)S(1)}, s32[16]{0:T(128)}, u32[]{:S(2)}) copy-start(s32[16]{0:T(128)} %param.19) | copy-start | bytes 196
Sparse Core Ops, SparseCore 0:
  9.1 38.4 all-gather.3
where the time goes:
time: 461 us; the launch traced here: 459 us
  blocking collectives  269 us (58%)
  matrix products  56.8 us (12%)
  loops' own time  40.5 us (9%)
  local copies, waits for them, and re-layouts  37.2 us (8%)
  other arithmetic  24.1 us (5%)
  starting transfers between devices  14.8 us (3%)
  between operations  13.5 us (3%)
    psum x1, blocking collectives, shards(): in_sums = lax.psum((train_in_part, query_in_part), ROW)  81.4 us
    psum x1, blocking collectives, shards(): out_sums = lax.psum((train_out_part, query_out_part), COL)  74.4 us
    psum x5, blocking collectives, by_axis(): value = lax.psum(value, axis)  68.1 us
    dot_general x16, matrix products, per_query(): lax.dot_general(train_in_rot, scaled, (((1,), (1,)), ((), ())), preferred...  46.7 us
    another operation x1, loops' own time, shards(): partial_scores = lax.map(per_query, (query_starts, query_ends))  40.5 us
    all_gather x1, blocking collectives, gather_together(): lines, at, gathered = (lax.all_gather(line, axis), 0, [])  31.4 us
    and x16, other arithmetic, per_query(): inside = (positions >= span_start) & (positions < span_end)  19.6 us
    dynamic_slice x32, local copies, waits for them, and re-layouts, shards(): partial_scores = lax.map(per_query, (query_starts, query_ends))  19.4 us
  transfers between devices with their start and end apart: 4, of which 1 were waited for; matrix products, arithmetic and copies ran while one was open for 4% of the time, Pallas kernels for 0%

commit v1 on v0

--- a/solution.py
+++ b/solution.py
@@ -32,7 +32,7 @@
 
 def by_axis(value, axes):
     for axis in axes:
-        value = lax.psum(value, axis)
+        value = jnp.sum(lax.all_gather(value, axis), axis=0)
     return value
 
 

time: 461 us -> 444 us (0.963)
  blocking collectives: 269 us -> 252 us
    psum x5 -> x0, blocking collectives: 68.1 us -> none  [by_axis(): value = lax.psum(value, axis)]
    all_gather x0 -> x5, blocking collectives: none -> 51 us  [by_axis(): value = jnp.sum(lax.all_gather(value, axis), axis=0)]
where the time goes in v1:
time: 444 us; the launch traced here: 442 us
  blocking collectives  252 us (57%)
  matrix products  56.8 us (13%)
  loops' own time  40.5 us (9%)
  local copies, waits for them, and re-layouts  37.2 us (8%)
  other arithmetic  24.2 us (5%)
  starting transfers between devices  14.8 us (3%)
  between operations  13.5 us (3%)
    psum x1, blocking collectives, shards(): in_sums = lax.psum((train_in_part, query_in_part), ROW)  81.4 us
    psum x1, blocking collectives, shards(): out_sums = lax.psum((train_out_part, query_out_part), COL)  74.4 us
    all_gather x5, blocking collectives, by_axis(): value = jnp.sum(lax.all_gather(value, axis), axis=0)  51 us
    dot_general x16, matrix products, per_query(): lax.dot_general(train_in_rot, scaled, (((1,), (1,)), ((), ())), preferred...  46.7 us
    another operation x1, loops' own time, shards(): partial_scores = lax.map(per_query, (query_starts, query_ends))  40.5 us
    all_gather x1, blocking collectives, gather_together(): lines, at, gathered = (lax.all_gather(line, axis), 0, [])  31.4 us
    and x16, other arithmetic, per_query(): inside = (positions >= span_start) & (positions < span_end)  19.6 us
    dynamic_slice x32, local copies, waits for them, and re-layouts, shards(): partial_scores = lax.map(per_query, (query_starts, query_ends))  19.4 us
  transfers between devices with their start and end apart: 4, of which 1 were waited for; matrix products, arithmetic and copies ran while one was open for 4% of the time, Pallas kernels for 0%

profile of v1, /device:TPU:1, one launch (start us, length us, event | category | flops | bytes accessed | tf_op | source)
XLA Modules:
  0.0 441.5 jit_solution(11337243910885903842)
XLA Ops:
  6.5 0.9 copy.31
  7.5 0.8 copy.32
  8.2 0.6 pad_maximum_fusion.1
  8.9 13.6 %all_to_all.70 = bf16[2,16,512]{2,0,1:T(2,128)(2,1)S(1)} all-to-all(bf16[2,16,512]{2,0,1:T(2,128)(2,1)} %bitcast.64), channel_id=1, replica_groups=mesh['row_0'=4,'row_1'=2,'col_0'=2,'col_1'=4,'col_2'=2] {'col_0','col_1'..., dimensions={1} | all-to-all | bytes 65536 | tf_op jit(solution)/shard_map/all_to_all | solution.py:57
  22.6 3.7 all-to-all-start
  26.2 3.2 broadcast_add_fusion
  29.5 2.7 all-to-all-done
  32.2 31.4 %all-gather = bf16[393216]{0:T(1024)(128)(2,1)S(1)} all-gather(bf16[49152]{0:T(1024)(128)(2,1)S(1)} %pad_maximum_fusion), channel_id=2, replica_groups=mesh['row_0'=4,'row_1'=2,'col_0'=2,'col_1'=4,'col_2'=2] {'row_0','row_1'}, dimensions={0}, use_global_device_ids=true | all-gather | bytes 884736 | tf_op jit(solution)/shard_map/all_gather | solution.py:25
  64.0 1.0 reshape_reshape.9
  65.0 1.8 reshape.40
  66.9 0.9 slice.17
  67.7 1.3 all_to_all.58
  69.0 1.1 copy.26
  70.1 4.5 %all-to-all-start.2 = ((bf16[32,8,1024]{2,0,1:T(8,128)(2,1)}), bf16[32,8,1024]{2,0,1:T(8,128)(2,1)}, u32[]{:S(2)}, u32[]{:S(2)}) async-start(bf16[32,8,1024]{2,0,1:T(8,128)(2,1)} %copy.26), calls=%async_computation.2 | async-start | bytes 1048576 | tf_op jit(solution)/shard_map/all_to_all | solution.py:53
  74.7 1.8 fusion.18
  76.4 0.8 reshape_reshape.8
  77.3 2.5 fusion.15
  79.7 1.1 slice.18
  80.8 2.3 all_to_all.62
  83.1 2.8 copy.27
  85.9 6.6 %all-to-all-start.3 = ((bf16[64,8,1024]{2,0,1:T(8,128)(2,1)}), bf16[64,8,1024]{2,0,1:T(8,128)(2,1)}, u32[]{:S(2)}, u32[]{:S(2)}) async-start(bf16[64,8,1024]{2,0,1:T(8,128)(2,1)} %copy.27), calls=%async_computation.3 | async-start | bytes 2097152 | tf_op jit(solution)/shard_map/all_to_all | solution.py:52
  92.6 74.4 %all-reduce.4 = (bf16[256,1024]{1,0:T(8,128)(2,1)}, bf16[512,1024]{1,0:T(8,128)(2,1)}) all-reduce(f32[256,1024]{1,0:T(8,128)} %fusion.15, f32[512,1024]{1,0:T(8,128)S(1)} %fusion.18), channel_id=1, replica_groups=mesh['row_0'=4,'row_1'=2,'col_0'=2,'col_1'=4,'col_2'=2] {'col_0','col_1'..., use_global_device_ids=true, to_apply=%region_0.0 | all-reduce | flops 786432 | bytes 4718592 | tf_op jit(solution)/shard_map/psum | solution.py:65
  166.9 1.5 copy.28
  168.4 2.6 fusion.16
  171.0 3.3 fusion.17
  174.3 81.4 %all-reduce.5 = (bf16[256,512]{1,0:T(8,128)(2,1)}, bf16[512,512]{1,0:T(8,128)(2,1)}) all-reduce(f32[256,512]{1,0:T(8,128)} %fusion.16, f32[512,512]{1,0:T(8,128)} %fusion.17), channel_id=1, replica_groups=mesh['row_0'=4,'row_1'=2,'col_0'=2,'col_1'=4,'col_2'=2] {'row_0','row_1'}, use_global_device_ids=true, to_apply=%region_1.0 | all-reduce | flops 393216 | bytes 2359296 | tf_op jit(solution)/shard_map/psum | solution.py:64
  255.7 127.2 %while.12 = (s32[]{:T(128)}, f32[16,512]{1,0:T(8,128)S(1)}, s32[16]{0:T(128)S(1)}, s32[16]{0:T(128)S(1)}, bf16[256,1024]{1,0:T(8,128)(2,1)}, /*index=5*/bf16[256...) while((s32[]{:T(128)}, f32[16,512]{1,0:T(8,128)S(1)}, ...), condition=%wide.region_6.7_spmd, body=%wide.region_4.6_spmd.sunk | while | flops 673316864 | bytes 5119617 | solution.py:90
  259.4 1.2 compare_and_fusion.2
  260.6 2.9 fusion.35
  267.4 1.2 compare_and_fusion.2
  268.6 2.9 fusion.35
  275.3 1.2 compare_and_fusion.2
  276.6 2.9 fusion.35
  283.3 1.2 compare_and_fusion.2
  284.5 2.9 fusion.35
  291.2 1.2 compare_and_fusion.2
  292.5 2.9 fusion.35
  299.2 1.2 compare_and_fusion.2
  300.4 2.9 fusion.35
  307.1 1.2 compare_and_fusion.2
  308.4 2.9 fusion.35
  315.1 1.2 compare_and_fusion.2
  316.3 2.9 fusion.35
  323.0 1.2 compare_and_fusion.2
  324.3 2.9 fusion.35
  331.0 1.2 compare_and_fusion.2
  332.2 2.9 fusion.35
  338.9 1.2 compare_and_fusion.2
  340.2 2.9 fusion.35
  346.9 1.2 compare_and_fusion.2
  348.1 2.9 fusion.35
  354.9 1.2 compare_and_fusion.2
  356.1 2.9 fusion.35
  362.8 1.2 compare_and_fusion.2
  364.0 2.9 fusion.35
  370.8 1.2 compare_and_fusion.2
  372.0 2.9 fusion.35
  378.7 1.2 compare_and_fusion.2
  380.0 2.9 fusion.35
  383.0 9.1 %all-gather.2 = f32[64,512]{1,0:T(8,128)S(1)} all-gather(f32[16,512]{1,0:T(8,128)S(1)} %get-tuple-element.119), channel_id=4, replica_groups=mesh['row_0'=4,'row_1'=2,'col_0'=2,'col_1'=4,'col_2'=2] {'row_0'}, dimensions={0}, use_global_device_ids=true | all-gather | bytes 163840 | tf_op jit(solution)/shard_map/all_gather | solution.py:35
  392.1 4.9 %all-gather.3 = f32[32,512]{1,0:T(8,128)S(1)} all-gather(f32[16,512]{1,0:T(8,128)S(1)} %reduce_sum.57), channel_id=5, replica_groups=mesh['row_0'=4,'row_1'=2,'col_0'=2,'col_1'=4,'col_2'=2] {'row_1'}, dimensions={0}, use_global_device_ids=true | all-gather | bytes 98304 | tf_op jit(solution)/shard_map/all_gather | solution.py:35
  397.0 3.4 all-gather.4
  400.5 13.7 %all-gather.5 = f32[64,512]{1,0:T(8,128)S(1)} all-gather(f32[16,512]{1,0:T(8,128)S(1)} %reduce_sum.59), channel_id=7, replica_groups=mesh['row_0'=4,'row_1'=2,'col_0'=2,'col_1'=4,'col_2'=2] {'col_1'}, dimensions={0}, use_global_device_ids=true | all-gather | bytes 163840 | tf_op jit(solution)/shard_map/all_gather | solution.py:35
  414.2 19.8 %all-gather.6 = f32[32,512]{1,0:T(8,128)S(1)} all-gather(f32[16,512]{1,0:T(8,128)S(1)} %reduce_sum.60), channel_id=8, replica_groups=mesh['row_0'=4,'row_1'=2,'col_0'=2,'col_1'=4,'col_2'=2] {'col_2'}, dimensions={0}, use_global_device_ids=true | all-gather | bytes 98304 | tf_op jit(solution)/shard_map/all_gather | solution.py:35
  (79 shorter events, 21.6 us)
Async XLA Ops:
  6.5 68.1 %copy-start = (bf16[512,1024]{1,0:T(8,128)(2,1)S(1)}, bf16[512,1024]{1,0:T(8,128)(2,1)}, u32[]{:S(2)}) copy-start(bf16[512,1024]{1,0:T(8,128)(2,1)} %param.16) | copy-start | bytes 3145732
  6.5 58.5 %all-gather.9.cloned.1.call-start = ((), (), s32[]{:S(2)}) async-start(), calls=%async_computation.4 | async-start | bytes 1671168 | tf_op jit(solution)/shard_map/all_gather | solution.py:25
  22.6 9.6 %all-to-all-start = ((bf16[4,16,512]{2,0,1:T(4,128)(2,1)}), bf16[4,16,512]{2,0,1:T(4,128)(2,1)S(1)}, u32[]{:S(2)}, u32[]{:S(2)}) async-start(bf16[4,16,512]{2,0,1:T(4,128)(2,1)} %bitcast.61), calls=%async_computation | async-start | bytes 131072 | tf_op jit(solution)/shard_map/all_to_all | solution.py:56
  63.9 1.1 copy-start.3
  66.8 3.3 copy-start.1
  70.1 6.3 %slice-start = ((bf16[8,49152]{1,0:T(8,128)(2,1)}), bf16[8,16384]{1,0:T(8,128)(2,1)S(1)}, s32[]{:S(2)}) async-start(bf16[8,49152]{1,0:T(8,128)(2,1)} %copy-done.3), calls=%async_computation.5 | async-start | bytes 524288 | tf_op jit(solution)/shard_map/slice | solution.py:27
  70.1 15.8 %all-to-all-start.2 = ((bf16[32,8,1024]{2,0,1:T(8,128)(2,1)}), bf16[32,8,1024]{2,0,1:T(8,128)(2,1)}, u32[]{:S(2)}, u32[]{:S(2)}) async-start(bf16[32,8,1024]{2,0,1:T(8,128)(2,1)} %copy.26), calls=%async_computation.2 | async-start | bytes 1048576 | tf_op jit(solution)/shard_map/all_to_all | solution.py:53
  77.2 2.5 copy-start.2
  85.9 85.1 %all-to-all-start.3 = ((bf16[64,8,1024]{2,0,1:T(8,128)(2,1)}), bf16[64,8,1024]{2,0,1:T(8,128)(2,1)}, u32[]{:S(2)}, u32[]{:S(2)}) async-start(bf16[64,8,1024]{2,0,1:T(8,128)(2,1)} %copy.27), calls=%async_computation.3 | async-start | bytes 2097152 | tf_op jit(solution)/shard_map/all_to_all | solution.py:52
  171.0 84.7 %copy-start.4 = (s32[16]{0:T(128)S(1)}, s32[16]{0:T(128)}, u32[]{:S(2)}) copy-start(s32[16]{0:T(128)} %param.18) | copy-start | bytes 196
  171.0 84.7 %copy-start.5 = (s32[16]{0:T(128)S(1)}, s32[16]{0:T(128)}, u32[]{:S(2)}) copy-start(s32[16]{0:T(128)} %param.19) | copy-start | bytes 196
Sparse Core Ops, SparseCore 0:
  9.1 38.4 all-gather.8
